TPU v7x, 128 devices: a whole 4x4x4 slice. The times are simulated.
128 devices in a mesh: dom: 16 (over y_hi, x, core), feat: 8 (over z, y_lo).
Axes of the slice: x: 4, y: 4 (y_hi: 2, y_lo: 2; y = y_hi * 2 + y_lo), z: 4, core: 2. Of those that a mesh axis runs over, the one named last changes fastest.
Arguments:
- state: bfloat16 [512, 32768], P('feat', 'dom'), may hold values from -3 to 3
- inputs: bfloat16 [2, 32768], P(None, 'dom'), may hold values from -6 to 6
- adj_tiles: bfloat16 [256, 4, 128, 128], P('dom'), may hold values from -0.25 to 0.25
- adj_cols: int32 [256, 4], P('dom'), may hold values from 0 to 17, as said below
- valid_rows: int32 [16], P('dom'), may hold values from 1024 to 2048, as said below
- cluster_of: int32 [32768], P('dom'), may hold values from 0 to 4095
- w_gates: bfloat16 [3, 512, 4, 512], P(None, 'feat'), may hold values from -0.125 to 0.125
- w_input: bfloat16 [3, 512, 2], P(None, 'feat'), may hold values from -4 to 4
- bias: float32 [3, 512], P(None, 'feat'), may hold values from -4 to 4
- w_value: bfloat16 [8, 64, 64], P('feat'), may hold values from -0.75 to 0.75
- source_emb: float32 [8, 10, 4096], P('feat'), may hold values from -5 to 5
- target_emb: float32 [8, 10, 4096], P('feat'), may hold values from -5 to 5
- coarse_tiles: bfloat16 [32, 2, 128, 128], replicated, may hold values from -0.375 to 0.375
- coarse_cols: int32 [32, 2], replicated, may hold values from 0 to 31
Outputs:
- new_state: bfloat16 [512, 32768], P('feat', 'dom')
Inputs may be any that keep to these rules, and one draw needn't show every extreme that they name: `adj_cols`: for local row tile t of a partition (t counted from 0 in the partition), every entry lies in t to t + 2, the first is t and the last is t + 2. `valid_rows`: some partition has all 2048 rows valid and another exactly half of them.
All inputs are finite; a program needn't handle non-finite values.
Results may differ from a plain program's by a relative error of at most 0.003.
Values may be sent and summed in bfloat16 or wider, within the bound.
A program may use at most 64 MiB of HBM per device.

v0:
```python
import math
import jax
import jax.numpy as jnp
from jax import lax
from jax.sharding import PartitionSpec as P


def extended_2(array, sides, width):
    for axis, dim in sides:
        peers, length = (lax.axis_size(axis), array.shape[dim])
        up = [(i, (i + 1) % peers) for i in range(peers)]
        down = [(j, i) for i, j in up]
        last = lax.slice_in_dim(array, length - width, length, axis=dim)
        leading = lax.slice_in_dim(array, 0, width, axis=dim)
        before = lax.ppermute(last, axis, up)
        after = lax.ppermute(leading, axis, down)
        array = jnp.concatenate([before, array, after], axis=dim)
    return array


def diffuse(states, adj_tiles, adj_cols, row_mask):
    tile_size = adj_tiles.shape[2]
    channels, row_count = states.shape
    extended = extended_2(states, (("dom", 1),), tile_size)
    extended = extended.reshape(channels, row_count // tile_size + 2, tile_size)
    picked = extended[:, adj_cols]
    result = jnp.einsum("hnkj,nkji->hni", picked, adj_tiles, preferred_element_type=jnp.float32)
    return (result.reshape(channels, row_count) * row_mask).astype(jnp.bfloat16)


def project(pooled, w_value):
    heads_here, head_size = (w_value.shape[0], w_value.shape[1])
    grouped = pooled.reshape(heads_here, head_size, pooled.shape[1])
    return jnp.einsum(
        "hde,hec->hdc", w_value.astype(jnp.float32), grouped, precision=lax.Precision.HIGHEST
    ).astype(jnp.bfloat16)


def attend(source_cols, target_emb, values):
    heads_here, emb_dim, query_count = source_cols.shape
    block_rows = math.gcd(query_count, 512)
    blocks = source_cols.reshape(heads_here, emb_dim, query_count // block_rows, block_rows)
    blocks = jnp.moveaxis(blocks, 2, 0)

    def one_block(source_block):
        scores = jnp.einsum(
            "hei,hej->hij", source_block, target_emb, precision=lax.Precision.HIGHEST
        )
        scores = jnp.maximum(scores, 0.0)
        row_peak = jnp.max(scores, axis=2, keepdims=True)
        raised = jnp.exp(scores - row_peak)
        weights = (raised / jnp.sum(raised, axis=2, keepdims=True)).astype(jnp.bfloat16)
        return jnp.einsum("hdj,hij->hdi", values, weights, preferred_element_type=jnp.float32)

    outputs = lax.map(one_block, blocks)
    outputs = jnp.moveaxis(outputs, 0, 2)
    return outputs.reshape(heads_here, values.shape[1], query_count)


def body(
    state,
    inputs,
    adj_tiles,
    adj_cols,
    valid_rows,
    cluster_of,
    w_gates,
    w_input,
    bias,
    w_value,
    source_emb,
    target_emb,
    coarse_tiles,
    coarse_cols,
):
    channels, row_count = state.shape
    cluster_count = source_emb.shape[2]
    row_mask = (jnp.arange(row_count, dtype=jnp.int32) < valid_rows[0]).astype(jnp.float32)
    masked = (state.astype(jnp.float32) * row_mask).astype(jnp.bfloat16)
    hop_one = diffuse(masked, adj_tiles, adj_cols, row_mask)
    hop_two = diffuse(hop_one, adj_tiles, adj_cols, row_mask)
    member = (cluster_of[:, None] == jnp.arange(cluster_count, dtype=jnp.int32)[None, :]).astype(
        jnp.bfloat16
    )
    cluster_sums = jnp.dot(masked, member, preferred_element_type=jnp.float32)
    counts = jnp.dot(
        row_mask.astype(jnp.bfloat16)[None, :], member, preferred_element_type=jnp.float32
    )
    cluster_sums, counts = (
        lax.psum(cluster_sums.astype(jnp.bfloat16), "dom").astype(jnp.float32),
        lax.psum(counts.astype(jnp.bfloat16), "dom").astype(jnp.float32),
    )
    pooled = cluster_sums / jnp.maximum(counts, 1.0)
    all_values = project(pooled, w_value)
    attended = attend(source_emb, target_emb, all_values)
    coarse_attn = (pooled + attended.reshape(channels, cluster_count)).astype(jnp.bfloat16)
    tile_size = coarse_tiles.shape[2]
    coarse_grid = coarse_attn.reshape(channels, cluster_count // tile_size, tile_size)
    picked = coarse_grid[:, coarse_cols]
    coarse_terms = jnp.einsum(
        "hnkj,nkji->hni", picked, coarse_tiles, preferred_element_type=jnp.float32
    )
    coarse = (
        coarse_attn.astype(jnp.float32) + coarse_terms.reshape(channels, cluster_count)
    ).astype(jnp.bfloat16)
    unpooled = jnp.take(coarse, cluster_of, axis=1)
    features = jnp.stack([masked, hop_one, hop_two, unpooled])
    gate_sums = jnp.einsum(
        "ghkc,kcr->ghr",
        w_gates,
        lax.all_gather(features, "feat", axis=1, tiled=True),
        preferred_element_type=jnp.float32,
    )
    input_terms = (
        jnp.einsum("ghf,fr->ghr", w_input, inputs, preferred_element_type=jnp.float32)
        + bias[:, :, None]
    )
    update = jax.nn.sigmoid(input_terms[0] + gate_sums[0])
    reset = jax.nn.sigmoid(input_terms[1] + gate_sums[1])
    candidate = jnp.tanh(input_terms[2] + reset * gate_sums[2])
    fresh_state = (update * masked.astype(jnp.float32) + (1.0 - update) * candidate) * row_mask
    return fresh_state.astype(jnp.bfloat16)


def solution(mesh):
    return jax.shard_map(
        body,
        mesh=mesh,
        in_specs=(
            P("feat", "dom"),
            P(None, "dom"),
            P("dom", None, None, None),
            P("dom", None),
            P("dom"),
            P("dom"),
            P(None, "feat", None, None),
            P(None, "feat", None),
            P(None, "feat"),
            P("feat", None, None),
            P("feat", None, None),
            P("feat", None, None),
            P(),
            P(),
        ),
        out_specs=P("feat", "dom"),
        check_vma=False,
    )
```

profile of v0, /device:TPU:1, one launch (start us, length us, event | category | flops | bytes accessed | tf_op | source)
XLA Modules:
  0.0 465.0 jit_solution(15305916377223197281)
XLA Ops:
  8.4 8.4 %fusion.15 = bf16[64,4096]{1,0:T(8,128)(2,1)} fusion(bf16[64,2048]{1,0:T(8,128)(2,1)S(1)} %multiply_convert_fusion.2, s32[2048]{0:T(1024)} %param.21), kind=kOutput, calls=%fused_computation.25 | convolution fusion | flops 1082392576 | bytes 794624 | tf_op jit(solution)/shard_map/dot_general | solution.py:85
  21.8 6.0 %fusion.9 = f32[1,4096]{1,0:T(1,128)S(1)} fusion(bf16[2048,1]{0,1:T(2,128)(2,1)S(1)} %reshape.241, s32[2048]{0:T(1024)S(1)} %copy-done.7), kind=kOutput, calls=%fused_computation.19 | convolution fusion | flops 25165824 | bytes 28672 | tf_op jit(solution)/shard_map/dot_general | solution.py:86
  27.9 67.7 %psum.15 = bf16[1,4096]{1,0:T(2,128)(2,1)S(1)} all-reduce(bf16[1,4096]{1,0:T(2,128)(2,1)S(1)} %convert_element_type.97), channel_id=1, replica_groups=mesh['dom'=16,'feat'=8] {'dom'}, use_global_device_ids=true, to_apply=%region_1.0 | all-reduce | flops 4096 | bytes 16384 | tf_op jit(solution)/shard_map/psum | solution.py:91
  100.3 5.9 %collective-permute-start.3 = (bf16[64,128]{1,0:T(8,128)(2,1)S(1)}, bf16[64,128]{1,0:T(8,128)(2,1)S(1)}, u32[]{:S(2)}, u32[]{:S(2)}) collective-permute-start(bf16[64,128]{1,0:T(8,128)(2,1)S(1)} %get-tuple-element.51), channel_id=1, source_target_pairs={{8,0},{16,8},{24,16},{32,24},{40,32},{48,40},{56,48},{64,56},{72,6... | collective-permute-start | bytes 49160 | tf_op jit(solution)/shard_map/ppermute | solution.py:16
  118.0 41.8 %all-reduce.2.cloned.1.call-done = bf16[64,4096]{1,0:T(8,128)(2,1)} async-done(((bf16[64,4096]{1,0:T(8,128)(2,1)}), bf16[64,4096]{1,0:T(8,128)(2,1)}) %all-reduce.2.cloned.1.call-update) | async-done | bytes 524304 | tf_op jit(solution)/shard_map/psum | solution.py:90
  162.4 100.1 %while.10 = (s32[]{:T(128)}, f32[8,1,64,512]{3,2,1,0:T(8,128)}, f32[8,1,10,512]{3,0,1,2:T(8,128)}, f32[1,10,4096]{2,0,1:T(1,128)S(1)}, bf16[1,64,4096]{2,1,0:T(8,128)(2,1)}, /*index=5*/s32[]{:T(128)}) while((s32[]{:T(128)}, f32[8,1,64,512]{3,2,1,0:T(8,128)}, f32[8,1,10,512]{3,0,1,2:T(8,128)}, f32[1,10,4096]{2,0,1:T(1,128)S(1)}, ...), condition=%wide.region_5.6_spmd, body=%wide.region_2.5_spmd.sunk | while | flops 538967040 | bytes 28153968 | solution.py:55
  163.4 7.2 %maximum_reduce_fusion.2 = (f32[512]{0:T(512)S(1)}, f32[512,4096]{1,0:T(8,128)S(1)}) fusion(f32[1,10,4096]{2,0,1:T(1,128)S(1)} %get-tuple-element.108, f32[1,1,10,512]{3,0,1,2:T(1,128)S(1)} %constant_dynamic-slice_fusion.2), kind=kOutput, calls=%fused_computation.6.clone.1 | convolution fusion | flops 255852032 | bytes 8574976 | tf_op jit(solution)/shard_map/while/body/eval_jaxpr/hei,hej->hij/dot_general | solution.py:46
  172.1 2.9 fusion.65
  175.9 7.2 %maximum_reduce_fusion.2 = (f32[512]{0:T(512)S(1)}, f32[512,4096]{1,0:T(8,128)S(1)}) fusion(f32[1,10,4096]{2,0,1:T(1,128)S(1)} %get-tuple-element.108, f32[1,1,10,512]{3,0,1,2:T(1,128)S(1)} %constant_dynamic-slice_fusion.2), kind=kOutput, calls=%fused_computation.6.clone.1 | convolution fusion | flops 255852032 | bytes 8574976 | tf_op jit(solution)/shard_map/while/body/eval_jaxpr/hei,hej->hij/dot_general | solution.py:46
  184.6 2.9 fusion.65
  188.4 7.2 %maximum_reduce_fusion.2 = (f32[512]{0:T(512)S(1)}, f32[512,4096]{1,0:T(8,128)S(1)}) fusion(f32[1,10,4096]{2,0,1:T(1,128)S(1)} %get-tuple-element.108, f32[1,1,10,512]{3,0,1,2:T(1,128)S(1)} %constant_dynamic-slice_fusion.2), kind=kOutput, calls=%fused_computation.6.clone.1 | convolution fusion | flops 255852032 | bytes 8574976 | tf_op jit(solution)/shard_map/while/body/eval_jaxpr/hei,hej->hij/dot_general | solution.py:46
  197.1 2.9 fusion.65
  200.9 7.2 %maximum_reduce_fusion.2 = (f32[512]{0:T(512)S(1)}, f32[512,4096]{1,0:T(8,128)S(1)}) fusion(f32[1,10,4096]{2,0,1:T(1,128)S(1)} %get-tuple-element.108, f32[1,1,10,512]{3,0,1,2:T(1,128)S(1)} %constant_dynamic-slice_fusion.2), kind=kOutput, calls=%fused_computation.6.clone.1 | convolution fusion | flops 255852032 | bytes 8574976 | tf_op jit(solution)/shard_map/while/body/eval_jaxpr/hei,hej->hij/dot_general | solution.py:46
  209.6 2.9 fusion.65
  213.4 7.2 %maximum_reduce_fusion.2 = (f32[512]{0:T(512)S(1)}, f32[512,4096]{1,0:T(8,128)S(1)}) fusion(f32[1,10,4096]{2,0,1:T(1,128)S(1)} %get-tuple-element.108, f32[1,1,10,512]{3,0,1,2:T(1,128)S(1)} %constant_dynamic-slice_fusion.2), kind=kOutput, calls=%fused_computation.6.clone.1 | convolution fusion | flops 255852032 | bytes 8574976 | tf_op jit(solution)/shard_map/while/body/eval_jaxpr/hei,hej->hij/dot_general | solution.py:46
  225.9 7.2 %maximum_reduce_fusion.2 = (f32[512]{0:T(512)S(1)}, f32[512,4096]{1,0:T(8,128)S(1)}) fusion(f32[1,10,4096]{2,0,1:T(1,128)S(1)} %get-tuple-element.108, f32[1,1,10,512]{3,0,1,2:T(1,128)S(1)} %constant_dynamic-slice_fusion.2), kind=kOutput, calls=%fused_computation.6.clone.1 | convolution fusion | flops 255852032 | bytes 8574976 | tf_op jit(solution)/shard_map/while/body/eval_jaxpr/hei,hej->hij/dot_general | solution.py:46
  234.6 2.9 fusion.65
  238.4 7.2 %maximum_reduce_fusion.2 = (f32[512]{0:T(512)S(1)}, f32[512,4096]{1,0:T(8,128)S(1)}) fusion(f32[1,10,4096]{2,0,1:T(1,128)S(1)} %get-tuple-element.108, f32[1,1,10,512]{3,0,1,2:T(1,128)S(1)} %constant_dynamic-slice_fusion.2), kind=kOutput, calls=%fused_computation.6.clone.1 | convolution fusion | flops 255852032 | bytes 8574976 | tf_op jit(solution)/shard_map/while/body/eval_jaxpr/hei,hej->hij/dot_general | solution.py:46
  247.1 2.9 fusion.65
  250.9 7.2 %maximum_reduce_fusion.2 = (f32[512]{0:T(512)S(1)}, f32[512,4096]{1,0:T(8,128)S(1)}) fusion(f32[1,10,4096]{2,0,1:T(1,128)S(1)} %get-tuple-element.108, f32[1,1,10,512]{3,0,1,2:T(1,128)S(1)} %constant_dynamic-slice_fusion.2), kind=kOutput, calls=%fused_computation.6.clone.1 | convolution fusion | flops 255852032 | bytes 8574976 | tf_op jit(solution)/shard_map/while/body/eval_jaxpr/hei,hej->hij/dot_general | solution.py:46
  259.6 2.9 fusion.65
  270.6 8.0 %gather_fusion.3 = bf16[2048,64]{1,0:T(8,128)(2,1)} fusion(bf16[64,4096]{0,1:T(8,128)(2,1)S(1)} %copy.39, s32[2048]{0:T(1024)S(1)} %fusion.43), kind=kCustom, calls=%fused_computation.3 | custom fusion | bytes 532480 | tf_op jit(solution)/shard_map/jit(_take)/gather | solution.py:106
  283.8 167.9 %all-gather.2.cloned.1.call-done = bf16[4,512,2048]{2,1,0:T(8,128)(2,1)} async-done(((bf16[4,64,2048]{2,1,0:T(8,128)(2,1)}), bf16[4,512,2048]{2,1,0:T(8,128)(2,1)}) %all-gather.2.cloned.1.call-update) | async-done | bytes 8388624 | tf_op jit(solution)/shard_map/all_gather | solution.py:111
  451.7 5.4 %fusion.17 = f32[3,64,2048]{2,1,0:T(8,128)S(1)} fusion(bf16[4,512,2048]{2,1,0:T(8,128)(2,1)} %all-gather.2.cloned.1.call-done, bf16[3,64,4,512]{3,2,1,0:T(4,128)(2,1)} %param.22), kind=kOutput, calls=%fused_computation.28 | convolution fusion | flops 1610612736 | bytes 10747904 | tf_op jit(solution)/shard_map/ghkc,kcr->ghr/dot_general | solution.py:108
  (120 shorter events, 61.7 us)
Async XLA Ops:
  6.5 91.3 %copy-start = (bf16[16,4,128,128]{3,2,1,0:T(8,128)(2,1)S(1)}, bf16[16,4,128,128]{3,2,1,0:T(8,128)(2,1)}, u32[]{:S(2)}) copy-start(bf16[16,4,128,128]{3,2,1,0:T(8,128)(2,1)} %param.18) | copy-start | bytes 6291460
  6.5 13.3 %copy-start.3 = (bf16[64,2048]{1,0:T(8,128)(2,1)S(1)}, bf16[64,2048]{1,0:T(8,128)(2,1)}, u32[]{:S(2)}) copy-start(bf16[64,2048]{1,0:T(8,128)(2,1)} %param.16) | copy-start | bytes 786436
  6.5 13.3 %copy-start.7 = (s32[2048]{0:T(1024)S(1)}, s32[2048]{0:T(1024)}, u32[]{:S(2)}) copy-start(s32[2048]{0:T(1024)} %param.21) | copy-start | bytes 24580
  6.5 14.0 %copy-start.6 = (f32[1,10,4096]{2,0,1:T(1,128)S(1)}, f32[1,10,4096]{2,0,1:T(1,128)}, u32[]{:S(2)}) copy-start(f32[1,10,4096]{2,0,1:T(1,128)} %param.26) | copy-start | bytes 491524
  6.5 153.2 %all-reduce.2.cloned.1.call-start = ((), (), s32[]{:S(2)}) async-start(), calls=%async_computation | async-start | bytes 1048576 | tf_op jit(solution)/shard_map/psum | solution.py:90
  16.8 78.9 %copy-start.12 = (s32[32,2]{0,1:T(2,128)S(1)}, s32[32,2]{0,1:T(2,128)}, u32[]{:S(2)}) copy-start(s32[32,2]{0,1:T(2,128)} %param.29) | copy-start | bytes 772
  16.8 78.9 %copy-start.10 = (s32[16,4]{0,1:T(4,128)S(1)}, s32[16,4]{0,1:T(4,128)}, u32[]{:S(2)}) copy-start(s32[16,4]{0,1:T(4,128)} %param.19) | copy-start | bytes 772
  16.8 434.9 %all-gather.2.cloned.1.call-start = ((), (), s32[]{:S(2)}) async-start(), calls=%async_computation.1 | async-start | bytes 9437184 | tf_op jit(solution)/shard_map/all_gather | solution.py:111
  16.9 79.2 %collective-permute-start.1 = (bf16[64,128]{1,0:T(8,128)(2,1)S(1)}, bf16[64,128]{1,0:T(8,128)(2,1)S(1)}, u32[]{:S(2)}, u32[]{:S(2)}) collective-permute-start(bf16[64,128]{1,0:T(8,128)(2,1)S(1)} %get-tuple-element.53), channel_id=1, source_target_pairs={{8,0},{16,8},{24,16},{32,24},{40,32},{48,40},{56,48},{64,56},{72,6... | collective-permute-start | bytes 49160 | tf_op jit(solution)/shard_map/ppermute | solution.py:16
  18.3 77.7 %collective-permute-start = (bf16[64,128]{1,0:T(8,128)(2,1)S(1)}, bf16[64,128]{1,0:T(8,128)(2,1)S(1)}, u32[]{:S(2)}, u32[]{:S(2)}) collective-permute-start(bf16[64,128]{1,0:T(8,128)(2,1)S(1)} %get-tuple-element.52), channel_id=1, source_target_pairs={{0,8},{8,16},{16,24},{24,32},{32,40},{40,48},{48,56},{56,64},{64,7... | collective-permute-start | bytes 49160 | tf_op jit(solution)/shard_map/ppermute | solution.py:15
  97.8 62.0 %copy-start.13 = (bf16[1,64,64]{2,1,0:T(8,128)(2,1)S(1)}, bf16[1,64,64]{2,1,0:T(8,128)(2,1)}, u32[]{:S(2)}) copy-start(bf16[1,64,64]{2,1,0:T(8,128)(2,1)} %param.25) | copy-start | bytes 24580
  99.6 62.9 %copy-start.1 = (f32[1,10,4096]{2,0,1:T(1,128)S(1)}, f32[1,10,4096]{2,0,1:T(1,128)}, u32[]{:S(2)}) copy-start(f32[1,10,4096]{2,0,1:T(1,128)} %param.27) | copy-start | bytes 491524
  100.3 8.2 %collective-permute-start.3 = (bf16[64,128]{1,0:T(8,128)(2,1)S(1)}, bf16[64,128]{1,0:T(8,128)(2,1)S(1)}, u32[]{:S(2)}, u32[]{:S(2)}) collective-permute-start(bf16[64,128]{1,0:T(8,128)(2,1)S(1)} %get-tuple-element.51), channel_id=1, source_target_pairs={{8,0},{16,8},{24,16},{32,24},{40,32},{48,40},{56,48},{64,56},{72,6... | collective-permute-start | bytes 49160 | tf_op jit(solution)/shard_map/ppermute | solution.py:16
  106.3 2.3 collective-permute-start.2
  162.4 101.4 %copy-start.5 = (bf16[64,4096]{1,0:T(8,128)(2,1)S(1)}, bf16[64,4096]{1,0:T(8,128)(2,1)}, u32[]{:S(2)}) copy-start(bf16[64,4096]{1,0:T(8,128)(2,1)} %all-reduce.2.cloned.1.call-done) | copy-start | bytes 1572868
  163.4 8.7 %copy-start.14 = (bf16[1,64,4096]{2,1,0:T(8,128)(2,1)S(1)}, bf16[1,64,4096]{2,1,0:T(8,128)(2,1)}, u32[]{:S(2)}) copy-start(bf16[1,64,4096]{2,1,0:T(8,128)(2,1)} %get-tuple-element.109) | copy-start | bytes 1572868 | tf_op jit(solution)/shard_map/while
  175.9 8.7 %copy-start.14 = (bf16[1,64,4096]{2,1,0:T(8,128)(2,1)S(1)}, bf16[1,64,4096]{2,1,0:T(8,128)(2,1)}, u32[]{:S(2)}) copy-start(bf16[1,64,4096]{2,1,0:T(8,128)(2,1)} %get-tuple-element.109) | copy-start | bytes 1572868 | tf_op jit(solution)/shard_map/while
  188.4 8.7 %copy-start.14 = (bf16[1,64,4096]{2,1,0:T(8,128)(2,1)S(1)}, bf16[1,64,4096]{2,1,0:T(8,128)(2,1)}, u32[]{:S(2)}) copy-start(bf16[1,64,4096]{2,1,0:T(8,128)(2,1)} %get-tuple-element.109) | copy-start | bytes 1572868 | tf_op jit(solution)/shard_map/while
  213.4 8.7 %copy-start.14 = (bf16[1,64,4096]{2,1,0:T(8,128)(2,1)S(1)}, bf16[1,64,4096]{2,1,0:T(8,128)(2,1)}, u32[]{:S(2)}) copy-start(bf16[1,64,4096]{2,1,0:T(8,128)(2,1)} %get-tuple-element.109) | copy-start | bytes 1572868 | tf_op jit(solution)/shard_map/while
  238.4 8.7 %copy-start.14 = (bf16[1,64,4096]{2,1,0:T(8,128)(2,1)S(1)}, bf16[1,64,4096]{2,1,0:T(8,128)(2,1)}, u32[]{:S(2)}) copy-start(bf16[1,64,4096]{2,1,0:T(8,128)(2,1)} %get-tuple-element.109) | copy-start | bytes 1572868 | tf_op jit(solution)/shard_map/while
  250.9 8.7 %copy-start.14 = (bf16[1,64,4096]{2,1,0:T(8,128)(2,1)S(1)}, bf16[1,64,4096]{2,1,0:T(8,128)(2,1)}, u32[]{:S(2)}) copy-start(bf16[1,64,4096]{2,1,0:T(8,128)(2,1)} %get-tuple-element.109) | copy-start | bytes 1572868 | tf_op jit(solution)/shard_map/while
  264.1 18.0 %copy-start.8 = (bf16[2,2048]{1,0:T(2,128)(2,1)S(1)}, bf16[2,2048]{1,0:T(2,128)(2,1)}, u32[]{:S(2)}) copy-start(bf16[2,2048]{1,0:T(2,128)(2,1)} %param.17) | copy-start | bytes 24580
  264.1 18.0 %copy-start.9 = (f32[3,64]{1,0:T(4,128)S(1)}, f32[3,64]{1,0:T(4,128)}, u32[]{:S(2)}) copy-start(f32[3,64]{1,0:T(4,128)} %param.24) | copy-start | bytes 2308
  264.1 18.0 %copy-start.11 = (bf16[3,64,2]{1,2,0:T(2,128)(2,1)S(1)}, bf16[3,64,2]{1,2,0:T(2,128)(2,1)}, u32[]{:S(2)}) copy-start(bf16[3,64,2]{1,2,0:T(2,128)(2,1)} %param.23) | copy-start | bytes 2308
  (4 other events, 23.5 us)
Sparse Core Ops, SparseCore 0:
  16.9 142.7 all-reduce.1
  282.3 169.3 all-gather.1
where the time goes:
time: 466 us; the launch traced here: 465 us
  waiting for transfers between devices  210 us (45%)
  matrix products  110 us (24%)
  blocking collectives  67.7 us (15%)
  local copies, waits for them, and re-layouts  32 us (7%)
  other arithmetic  21.6 us (5%)
  between operations  14.5 us (3%)
  starting transfers between devices  8.94 us (2%)
    all_gather x1, waiting for transfers between devices, body(): lax.all_gather(features, 'feat', axis=1, tiled=True)  168 us
    psum x1, blocking collectives, body(): lax.psum(counts.astype(jnp.bfloat16), 'dom').astype(jnp.float32)  67.7 us
    dot_general x8, matrix products, one_block(): jnp.einsum('hei,hej->hij', source_block, target_emb, precision=lax.Precis...  57.3 us
    psum x1, waiting for transfers between devices, body(): lax.psum(cluster_sums.astype(jnp.bfloat16), 'dom').astype(jnp.float32)  41.8 us
    dot_general x8, matrix products, one_block(): jnp.einsum('hdj,hij->hdi', values, weights, preferred_element_type=jnp.fl...  23.1 us
    reduce_sum x8, other arithmetic, one_block(): jnp.sum(raised, axis=2, keepdims=True)  12 us
  transfers between devices with their start and end apart: 6, of which 2 were waited for; matrix products, arithmetic and copies ran while one was open for 5% of the time, Pallas kernels for 0%

commit v1 on v0

--- a/solution.py
+++ b/solution.py
@@ -3,6 +3,11 @@
 import jax.numpy as jnp
 from jax import lax
 from jax.sharding import PartitionSpec as P
+
+
+def gather_over(array, axis, dim):
+    sent = jnp.stack([array] * lax.axis_size(axis))
+    return jnp.concatenate(lax.all_to_all(sent, axis, 0, 0), axis=dim)
 
 
 def extended_2(array, sides, width):
@@ -108,7 +113,7 @@
     gate_sums = jnp.einsum(
         "ghkc,kcr->ghr",
         w_gates,
-        lax.all_gather(features, "feat", axis=1, tiled=True),
+        gather_over(features, "feat", 1),
         preferred_element_type=jnp.float32,
     )
     input_terms = (

time: 466 us -> 410 us (0.88)
  waiting for transfers between devices: 210 us -> 142 us
  local copies, waits for them, and re-layouts: 32 us -> 44 us
  starting transfers between devices: 8.94 us -> 14.1 us
    all_gather x1 -> x0, waiting for transfers between devices: 168 us -> none  [body(): lax.all_gather(features, 'feat', axis=1, tiled=True)]
    all_to_all x0 -> x1, waiting for transfers between devices: none -> 91.8 us  [gather_over(): return jnp.concatenate(lax.all_to_all(sent, axis, 0, 0), axis=dim)]
    reshape x0 -> x1, local copies, waits for them, and re-layouts: none -> 8.36 us  [gather_over(): return jnp.concatenate(lax.all_to_all(sent, axis, 0, 0), axis=dim)]
    psum x1, waiting for transfers between devices: 41.8 us -> 49.8 us  [body(): lax.psum(cluster_sums.astype(jnp.bfloat16), 'dom').astype(jnp.float32)]
    all_to_all x0 -> x1, starting transfers between devices: none -> 5.3 us  [gather_over(): return jnp.concatenate(lax.all_to_all(sent, axis, 0, 0), axis=dim)]
  transfers between devices with their start and end apart: 6 -> 6, of which waited for: 2 -> 2; matrix products, arithmetic and copies ran while one was open for 5% -> 8% of each run, Pallas kernels for 0% -> 0%
where the time goes in v1:
time: 410 us; the launch traced here: 409 us
  waiting for transfers between devices  142 us (35%)
  matrix products  110 us (27%)
  blocking collectives  63.5 us (15%)
  local copies, waits for them, and re-layouts  44 us (11%)
  other arithmetic  20.7 us (5%)
  between operations  14.5 us (4%)
  starting transfers between devices  14.1 us (3%)
    all_to_all x1, waiting for transfers between devices, gather_over(): return jnp.concatenate(lax.all_to_all(sent, axis, 0, 0), axis=dim)  91.8 us
    psum x1, blocking collectives, body(): lax.psum(counts.astype(jnp.bfloat16), 'dom').astype(jnp.float32)  63.5 us
    dot_general x8, matrix products, one_block(): jnp.einsum('hei,hej->hij', source_block, target_emb, precision=lax.Precis...  57.3 us
    psum x1, waiting for transfers between devices, body(): lax.psum(cluster_sums.astype(jnp.bfloat16), 'dom').astype(jnp.float32)  49.8 us
    dot_general x8, matrix products, one_block(): jnp.einsum('hdj,hij->hdi', values, weights, preferred_element_type=jnp.fl...  23.1 us
    reduce_sum x8, other arithmetic, one_block(): jnp.sum(raised, axis=2, keepdims=True)  12 us
    gather x2, local copies, waits for them, and re-layouts, body(): unpooled = jnp.take(coarse, cluster_of, axis=1)  9.23 us
    dot_general x1, matrix products, body(): cluster_sums = jnp.dot(masked, member, preferred_element_type=jnp.float32)  8.42 us
  transfers between devices with their start and end apart: 6, of which 2 were waited for; matrix products, arithmetic and copies ran while one was open for 8% of the time, Pallas kernels for 0%

profile of v1, /device:TPU:1, one launch (start us, length us, event | category | flops | bytes accessed | tf_op | source)
XLA Modules:
  0.0 408.8 jit_solution(9012399938136680418)
XLA Ops:
  11.1 8.4 %fusion.13 = bf16[64,4096]{1,0:T(8,128)(2,1)} fusion(bf16[64,2048]{1,0:T(8,128)(2,1)S(1)} %multiply_convert_fusion.2, s32[2048]{0:T(1024)} %param.21), kind=kOutput, calls=%fused_computation.23 | convolution fusion | flops 1082392576 | bytes 794624 | tf_op jit(solution)/shard_map/dot_general | solution.py:90
  20.5 6.2 %fusion.9 = f32[1,4096]{1,0:T(1,128)S(1)} fusion(bf16[2048,1]{0,1:T(2,128)(2,1)S(1)} %reshape.251, s32[2048]{0:T(1024)S(1)} %copy-done.7), kind=kOutput, calls=%fused_computation.19 | convolution fusion | flops 25165824 | bytes 28672 | tf_op jit(solution)/shard_map/dot_general | solution.py:91
  26.7 63.5 %psum.15 = bf16[1,4096]{1,0:T(2,128)(2,1)S(1)} all-reduce(bf16[1,4096]{1,0:T(2,128)(2,1)S(1)} %convert_element_type.97), channel_id=1, replica_groups=mesh['dom'=16,'feat'=8] {'dom'}, use_global_device_ids=true, to_apply=%region_1.0 | all-reduce | flops 4096 | bytes 16384 | tf_op jit(solution)/shard_map/psum | solution.py:96
  97.0 4.3 %collective-permute-start.3 = (bf16[64,128]{1,0:T(8,128)(2,1)S(1)}, bf16[64,128]{1,0:T(8,128)(2,1)S(1)}, u32[]{:S(2)}, u32[]{:S(2)}) collective-permute-start(bf16[64,128]{1,0:T(8,128)(2,1)S(1)} %get-tuple-element.56), channel_id=1, source_target_pairs={{8,0},{16,8},{24,16},{32,24},{40,32},{48,40},{56,48},{64,56},{72,6... | collective-permute-start | bytes 49160 | tf_op jit(solution)/shard_map/ppermute | solution.py:21
  113.0 49.8 %all-reduce.2.cloned.1.call-done = bf16[64,4096]{1,0:T(8,128)(2,1)} async-done(((bf16[64,4096]{1,0:T(8,128)(2,1)}), bf16[64,4096]{1,0:T(8,128)(2,1)}) %all-reduce.2.cloned.1.call-update) | async-done | bytes 524304 | tf_op jit(solution)/shard_map/psum | solution.py:95
  165.4 100.1 %while.10 = (s32[]{:T(128)}, f32[8,1,64,512]{3,2,1,0:T(8,128)}, f32[8,1,10,512]{3,0,1,2:T(8,128)}, f32[1,10,4096]{2,0,1:T(1,128)S(1)}, bf16[1,64,4096]{2,1,0:T(8,128)(2,1)}, /*index=5*/s32[]{:T(128)}) while((s32[]{:T(128)}, f32[8,1,64,512]{3,2,1,0:T(8,128)}, f32[8,1,10,512]{3,0,1,2:T(8,128)}, f32[1,10,4096]{2,0,1:T(1,128)S(1)}, ...), condition=%wide.region_5.6_spmd, body=%wide.region_2.5_spmd.sunk | while | flops 538967040 | bytes 28154468 | solution.py:60
  166.5 7.2 %maximum_reduce_fusion.2 = (f32[512]{0:T(512)S(1)}, f32[512,4096]{1,0:T(8,128)S(1)}) fusion(f32[1,10,4096]{2,0,1:T(1,128)S(1)} %get-tuple-element.113, f32[1,1,10,512]{3,0,1,2:T(1,128)S(1)} %constant_dynamic-slice_fusion.2), kind=kOutput, calls=%fused_computation.6.clone.1 | convolution fusion | flops 255852032 | bytes 8574976 | tf_op jit(solution)/shard_map/while/body/eval_jaxpr/hei,hej->hij/dot_general | solution.py:51
  175.1 2.9 fusion.61
  179.0 7.2 %maximum_reduce_fusion.2 = (f32[512]{0:T(512)S(1)}, f32[512,4096]{1,0:T(8,128)S(1)}) fusion(f32[1,10,4096]{2,0,1:T(1,128)S(1)} %get-tuple-element.113, f32[1,1,10,512]{3,0,1,2:T(1,128)S(1)} %constant_dynamic-slice_fusion.2), kind=kOutput, calls=%fused_computation.6.clone.1 | convolution fusion | flops 255852032 | bytes 8574976 | tf_op jit(solution)/shard_map/while/body/eval_jaxpr/hei,hej->hij/dot_general | solution.py:51
  187.6 2.9 fusion.61
  191.5 7.2 %maximum_reduce_fusion.2 = (f32[512]{0:T(512)S(1)}, f32[512,4096]{1,0:T(8,128)S(1)}) fusion(f32[1,10,4096]{2,0,1:T(1,128)S(1)} %get-tuple-element.113, f32[1,1,10,512]{3,0,1,2:T(1,128)S(1)} %constant_dynamic-slice_fusion.2), kind=kOutput, calls=%fused_computation.6.clone.1 | convolution fusion | flops 255852032 | bytes 8574976 | tf_op jit(solution)/shard_map/while/body/eval_jaxpr/hei,hej->hij/dot_general | solution.py:51
  204.0 7.2 %maximum_reduce_fusion.2 = (f32[512]{0:T(512)S(1)}, f32[512,4096]{1,0:T(8,128)S(1)}) fusion(f32[1,10,4096]{2,0,1:T(1,128)S(1)} %get-tuple-element.113, f32[1,1,10,512]{3,0,1,2:T(1,128)S(1)} %constant_dynamic-slice_fusion.2), kind=kOutput, calls=%fused_computation.6.clone.1 | convolution fusion | flops 255852032 | bytes 8574976 | tf_op jit(solution)/shard_map/while/body/eval_jaxpr/hei,hej->hij/dot_general | solution.py:51
  216.5 7.2 %maximum_reduce_fusion.2 = (f32[512]{0:T(512)S(1)}, f32[512,4096]{1,0:T(8,128)S(1)}) fusion(f32[1,10,4096]{2,0,1:T(1,128)S(1)} %get-tuple-element.113, f32[1,1,10,512]{3,0,1,2:T(1,128)S(1)} %constant_dynamic-slice_fusion.2), kind=kOutput, calls=%fused_computation.6.clone.1 | convolution fusion | flops 255852032 | bytes 8574976 | tf_op jit(solution)/shard_map/while/body/eval_jaxpr/hei,hej->hij/dot_general | solution.py:51
  229.0 7.2 %maximum_reduce_fusion.2 = (f32[512]{0:T(512)S(1)}, f32[512,4096]{1,0:T(8,128)S(1)}) fusion(f32[1,10,4096]{2,0,1:T(1,128)S(1)} %get-tuple-element.113, f32[1,1,10,512]{3,0,1,2:T(1,128)S(1)} %constant_dynamic-slice_fusion.2), kind=kOutput, calls=%fused_computation.6.clone.1 | convolution fusion | flops 255852032 | bytes 8574976 | tf_op jit(solution)/shard_map/while/body/eval_jaxpr/hei,hej->hij/dot_general | solution.py:51
  237.6 2.9 fusion.61
  241.5 7.2 %maximum_reduce_fusion.2 = (f32[512]{0:T(512)S(1)}, f32[512,4096]{1,0:T(8,128)S(1)}) fusion(f32[1,10,4096]{2,0,1:T(1,128)S(1)} %get-tuple-element.113, f32[1,1,10,512]{3,0,1,2:T(1,128)S(1)} %constant_dynamic-slice_fusion.2), kind=kOutput, calls=%fused_computation.6.clone.1 | convolution fusion | flops 255852032 | bytes 8574976 | tf_op jit(solution)/shard_map/while/body/eval_jaxpr/hei,hej->hij/dot_general | solution.py:51
  254.0 7.2 %maximum_reduce_fusion.2 = (f32[512]{0:T(512)S(1)}, f32[512,4096]{1,0:T(8,128)S(1)}) fusion(f32[1,10,4096]{2,0,1:T(1,128)S(1)} %get-tuple-element.113, f32[1,1,10,512]{3,0,1,2:T(1,128)S(1)} %constant_dynamic-slice_fusion.2), kind=kOutput, calls=%fused_computation.6.clone.1 | convolution fusion | flops 255852032 | bytes 8574976 | tf_op jit(solution)/shard_map/while/body/eval_jaxpr/hei,hej->hij/dot_general | solution.py:51
  262.6 2.9 fusion.61
  273.6 8.0 %gather_fusion.3 = bf16[2048,64]{1,0:T(8,128)(2,1)} fusion(bf16[64,4096]{0,1:T(8,128)(2,1)S(1)} %copy.53, s32[2048]{0:T(1024)S(1)} %fusion.38), kind=kCustom, calls=%fused_computation.3 | custom fusion | bytes 532480 | tf_op jit(solution)/shard_map/jit(_take)/gather | solution.py:111
  284.1 4.3 %stack.8 = bf16[8,4,64,2048]{3,2,1,0:T(8,128)(2,1)} broadcast(bf16[4,64,2048]{2,1,0:T(8,128)(2,1)S(1)} %pad_maximum_fusion), dimensions={1,2,3} | broadcast | bytes 9437184 | tf_op jit(solution)/shard_map/stack | solution.py:9
  288.5 5.3 %all-to-all-start = ((bf16[8,4,64,2048]{3,2,1,0:T(8,128)(2,1)}), bf16[8,4,64,2048]{3,2,1,0:T(8,128)(2,1)}, u32[]{:S(2)}, u32[]{:S(2)}) async-start(bf16[8,4,64,2048]{3,2,1,0:T(8,128)(2,1)} %stack.8), calls=%async_computation | async-start | bytes 16777216 | tf_op jit(solution)/shard_map/all_to_all | solution.py:10
  295.4 91.8 %all-to-all-done = bf16[8,4,64,2048]{3,2,1,0:T(8,128)(2,1)} async-done(((bf16[8,4,64,2048]{3,2,1,0:T(8,128)(2,1)}), bf16[8,4,64,2048]{3,2,1,0:T(8,128)(2,1)}, u32[]{:S(2)}, u32[]{:S(2)}) %all-to-all-start) | async-done | bytes 8388640 | tf_op jit(solution)/shard_map/all_to_all | solution.py:10
  387.2 8.4 %copy.55 = bf16[4,8,64,2048]{3,2,1,0:T(8,128)(2,1)} copy(bf16[4,8,64,2048]{3,2,0,1:T(8,128)(2,1)} %bitcast.32) | data formatting | bytes 16777216 | tf_op jit(solution)/shard_map/reshape | solution.py:10
  395.5 5.3 %convolution_bitcast_fusion = f32[3,64,2048]{2,1,0:T(8,128)S(1)} fusion(bf16[4,512,2048,1]{2,1,0,3:T(8,128)(2,1)} %bitcast.144, bf16[3,64,4,512]{3,2,1,0:T(4,128)(2,1)S(1)} %copy-done.13), kind=kOutput, calls=%fused_computation.26 | convolution fusion | flops 1610612736 | bytes 10747904 | tf_op jit(solution)/shard_map/ghkc,kcr->ghr/dot_general | solution.py:113
  (123 shorter events, 70.1 us)
Async XLA Ops:
  6.5 86.9 %copy-start = (bf16[16,4,128,128]{3,2,1,0:T(8,128)(2,1)S(1)}, bf16[16,4,128,128]{3,2,1,0:T(8,128)(2,1)}, u32[]{:S(2)}) copy-start(bf16[16,4,128,128]{3,2,1,0:T(8,128)(2,1)} %param.18) | copy-start | bytes 6291460
  6.5 13.0 %copy-start.3 = (bf16[64,2048]{1,0:T(8,128)(2,1)S(1)}, bf16[64,2048]{1,0:T(8,128)(2,1)}, u32[]{:S(2)}) copy-start(bf16[64,2048]{1,0:T(8,128)(2,1)} %param.16) | copy-start | bytes 786436
  6.5 13.0 %copy-start.7 = (s32[2048]{0:T(1024)S(1)}, s32[2048]{0:T(1024)}, u32[]{:S(2)}) copy-start(s32[2048]{0:T(1024)} %param.21) | copy-start | bytes 24580
  6.5 13.8 %copy-start.10 = (s32[16,4]{0,1:T(4,128)S(1)}, s32[16,4]{0,1:T(4,128)}, u32[]{:S(2)}) copy-start(s32[16,4]{0,1:T(4,128)} %param.19) | copy-start | bytes 772
  6.5 156.2 %all-reduce.2.cloned.1.call-start = ((), (), s32[]{:S(2)}) async-start(), calls=%async_computation.1 | async-start | bytes 1048576 | tf_op jit(solution)/shard_map/psum | solution.py:95
  8.4 83.3 %collective-permute-start = (bf16[64,128]{1,0:T(8,128)(2,1)S(1)}, bf16[64,128]{1,0:T(8,128)(2,1)S(1)}, u32[]{:S(2)}, u32[]{:S(2)}) collective-permute-start(bf16[64,128]{1,0:T(8,128)(2,1)S(1)} %get-tuple-element.57), channel_id=1, source_target_pairs={{0,8},{8,16},{16,24},{24,32},{32,40},{40,48},{48,56},{56,64},{64,7... | collective-permute-start | bytes 49160 | tf_op jit(solution)/shard_map/ppermute | solution.py:20
  11.1 79.2 %copy-start.6 = (f32[1,10,4096]{2,0,1:T(1,128)S(1)}, f32[1,10,4096]{2,0,1:T(1,128)}, u32[]{:S(2)}) copy-start(f32[1,10,4096]{2,0,1:T(1,128)} %param.26) | copy-start | bytes 491524
  11.1 80.6 %collective-permute-start.1 = (bf16[64,128]{1,0:T(8,128)(2,1)S(1)}, bf16[64,128]{1,0:T(8,128)(2,1)S(1)}, u32[]{:S(2)}, u32[]{:S(2)}) collective-permute-start(bf16[64,128]{1,0:T(8,128)(2,1)S(1)} %get-tuple-element.58), channel_id=1, source_target_pairs={{8,0},{16,8},{24,16},{32,24},{40,32},{48,40},{56,48},{64,56},{72,6... | collective-permute-start | bytes 49160 | tf_op jit(solution)/shard_map/ppermute | solution.py:21
  19.5 72.0 %copy-start.12 = (s32[32,2]{0,1:T(2,128)S(1)}, s32[32,2]{0,1:T(2,128)}, u32[]{:S(2)}) copy-start(s32[32,2]{0,1:T(2,128)} %param.29) | copy-start | bytes 772
  93.4 69.4 %copy-start.14 = (bf16[1,64,64]{2,1,0:T(8,128)(2,1)S(1)}, bf16[1,64,64]{2,1,0:T(8,128)(2,1)}, u32[]{:S(2)}) copy-start(bf16[1,64,64]{2,1,0:T(8,128)(2,1)} %param.25) | copy-start | bytes 24580
  95.2 70.3 %copy-start.1 = (f32[1,10,4096]{2,0,1:T(1,128)S(1)}, f32[1,10,4096]{2,0,1:T(1,128)}, u32[]{:S(2)}) copy-start(f32[1,10,4096]{2,0,1:T(1,128)} %param.27) | copy-start | bytes 491524
  95.3 8.3 %collective-permute-start.2 = (bf16[64,128]{1,0:T(8,128)(2,1)S(1)}, bf16[64,128]{1,0:T(8,128)(2,1)S(1)}, u32[]{:S(2)}, u32[]{:S(2)}) collective-permute-start(bf16[64,128]{1,0:T(8,128)(2,1)S(1)} %get-tuple-element.55), channel_id=1, source_target_pairs={{0,8},{8,16},{16,24},{24,32},{32,40},{40,48},{48,56},{56,64},{64,7... | collective-permute-start | bytes 49160 | tf_op jit(solution)/shard_map/ppermute | solution.py:20
  97.0 6.6 %collective-permute-start.3 = (bf16[64,128]{1,0:T(8,128)(2,1)S(1)}, bf16[64,128]{1,0:T(8,128)(2,1)S(1)}, u32[]{:S(2)}, u32[]{:S(2)}) collective-permute-start(bf16[64,128]{1,0:T(8,128)(2,1)S(1)} %get-tuple-element.56), channel_id=1, source_target_pairs={{8,0},{16,8},{24,16},{32,24},{40,32},{48,40},{56,48},{64,56},{72,6... | collective-permute-start | bytes 49160 | tf_op jit(solution)/shard_map/ppermute | solution.py:21
  165.4 101.4 %copy-start.5 = (bf16[64,4096]{1,0:T(8,128)(2,1)S(1)}, bf16[64,4096]{1,0:T(8,128)(2,1)}, u32[]{:S(2)}) copy-start(bf16[64,4096]{1,0:T(8,128)(2,1)} %all-reduce.2.cloned.1.call-done) | copy-start | bytes 1572868
  166.4 8.7 %copy-start.15 = (bf16[1,64,4096]{2,1,0:T(8,128)(2,1)S(1)}, bf16[1,64,4096]{2,1,0:T(8,128)(2,1)}, u32[]{:S(2)}) copy-start(bf16[1,64,4096]{2,1,0:T(8,128)(2,1)} %get-tuple-element.114) | copy-start | bytes 1572868 | tf_op jit(solution)/shard_map/while
  179.0 8.7 %copy-start.15 = (bf16[1,64,4096]{2,1,0:T(8,128)(2,1)S(1)}, bf16[1,64,4096]{2,1,0:T(8,128)(2,1)}, u32[]{:S(2)}) copy-start(bf16[1,64,4096]{2,1,0:T(8,128)(2,1)} %get-tuple-element.114) | copy-start | bytes 1572868 | tf_op jit(solution)/shard_map/while
  191.5 8.7 %copy-start.15 = (bf16[1,64,4096]{2,1,0:T(8,128)(2,1)S(1)}, bf16[1,64,4096]{2,1,0:T(8,128)(2,1)}, u32[]{:S(2)}) copy-start(bf16[1,64,4096]{2,1,0:T(8,128)(2,1)} %get-tuple-element.114) | copy-start | bytes 1572868 | tf_op jit(solution)/shard_map/while
  204.0 8.7 %copy-start.15 = (bf16[1,64,4096]{2,1,0:T(8,128)(2,1)S(1)}, bf16[1,64,4096]{2,1,0:T(8,128)(2,1)}, u32[]{:S(2)}) copy-start(bf16[1,64,4096]{2,1,0:T(8,128)(2,1)} %get-tuple-element.114) | copy-start | bytes 1572868 | tf_op jit(solution)/shard_map/while
  216.5 8.7 %copy-start.15 = (bf16[1,64,4096]{2,1,0:T(8,128)(2,1)S(1)}, bf16[1,64,4096]{2,1,0:T(8,128)(2,1)}, u32[]{:S(2)}) copy-start(bf16[1,64,4096]{2,1,0:T(8,128)(2,1)} %get-tuple-element.114) | copy-start | bytes 1572868 | tf_op jit(solution)/shard_map/while
  229.0 8.7 %copy-start.15 = (bf16[1,64,4096]{2,1,0:T(8,128)(2,1)S(1)}, bf16[1,64,4096]{2,1,0:T(8,128)(2,1)}, u32[]{:S(2)}) copy-start(bf16[1,64,4096]{2,1,0:T(8,128)(2,1)} %get-tuple-element.114) | copy-start | bytes 1572868 | tf_op jit(solution)/shard_map/while
  241.5 8.7 %copy-start.15 = (bf16[1,64,4096]{2,1,0:T(8,128)(2,1)S(1)}, bf16[1,64,4096]{2,1,0:T(8,128)(2,1)}, u32[]{:S(2)}) copy-start(bf16[1,64,4096]{2,1,0:T(8,128)(2,1)} %get-tuple-element.114) | copy-start | bytes 1572868 | tf_op jit(solution)/shard_map/while
  254.0 8.7 %copy-start.15 = (bf16[1,64,4096]{2,1,0:T(8,128)(2,1)S(1)}, bf16[1,64,4096]{2,1,0:T(8,128)(2,1)}, u32[]{:S(2)}) copy-start(bf16[1,64,4096]{2,1,0:T(8,128)(2,1)} %get-tuple-element.114) | copy-start | bytes 1572868 | tf_op jit(solution)/shard_map/while
  288.5 98.7 %all-to-all-start = ((bf16[8,4,64,2048]{3,2,1,0:T(8,128)(2,1)}), bf16[8,4,64,2048]{3,2,1,0:T(8,128)(2,1)}, u32[]{:S(2)}, u32[]{:S(2)}) async-start(bf16[8,4,64,2048]{3,2,1,0:T(8,128)(2,1)} %stack.8), calls=%async_computation | async-start | bytes 16777216 | tf_op jit(solution)/shard_map/all_to_all | solution.py:10
  387.2 8.4 %copy-start.13 = (bf16[3,64,4,512]{3,2,1,0:T(4,128)(2,1)S(1)}, bf16[3,64,4,512]{3,2,1,0:T(4,128)(2,1)}, u32[]{:S(2)}) copy-start(bf16[3,64,4,512]{3,2,1,0:T(4,128)(2,1)} %param.22) | copy-start | bytes 2359300
  (5 other events, 27.4 us)
Sparse Core Ops, SparseCore 0:
  19.6 143.1 all-reduce.1
